TPU v7x, 32 devices: a whole 2x2x4 slice. The times are simulated.
32 devices in a mesh: tile: 16 (over z, y, core), inner: 2 (over x).
Axes of the slice: x: 2, y: 2, z: 4, core: 2. Of those that a mesh axis runs over, the one named last changes fastest.
Arguments:
- amplitudes: bfloat16 [512, 4096], P('tile', 'inner'), may hold values from -6 to 6
- left_factors: bfloat16 [1024, 4096], P('tile', 'inner'), may hold values from -0.1875 to 0.1875
- right_factors: bfloat16 [1024, 16384], P(None, 'tile'), may hold values from -0.1875 to 0.1875
- tile_pattern: int32 [8, 32], replicated, may hold values from 0 to 1, as said below
- occupied_shift: float32 [512], P('inner'), may hold values from 0.5 to 2
- virtual_shift: float32 [16384], P('tile'), may hold values from 0.5 to 5
Outputs:
- residual: float32 [512, 16384], P('inner', 'tile')
Inputs may be any that keep to these rules, and one draw needn't show every extreme that they name: `tile_pattern`: 1 where the tiles interact, 0 where their integrals are dropped.
All inputs are finite; a program needn't handle non-finite values.
Results may differ from a plain program's by a relative error of at most 0.0029.
Values may be sent and summed in bfloat16 or wider, within the bound.
No kernel may reach another device: no remote copies, remote signals or barrier semaphores. Data moves between devices by JAX's collectives and lax.ppermute only.
A program may use at most 64 MiB of HBM per device.

v0:
```python
import functools

import jax
import jax.numpy as jnp
from jax import lax
from jax.experimental import pallas as pl
from jax.experimental.pallas import tpu as pltpu
from jax.sharding import PartitionSpec as P


TILE = 512
VMEM = pl.BlockSpec(memory_space=pltpu.VMEM)
SMEM = pl.BlockSpec(memory_space=pltpu.SMEM)
ANY = pl.BlockSpec(memory_space=pl.ANY)
PARAMS = pltpu.CompilerParams(vmem_limit_bytes=20 * 1024 * 1024)


def cost(flops, moved):
    return pl.CostEstimate(flops=int(flops), bytes_accessed=int(moved), transcendentals=0)


def keep_kernel(amplitudes, left, kept):
    rows = amplitudes.shape[0]
    kept[:rows, :] = amplitudes[...]
    kept[rows:, :] = left[...]


def place():
    t = lax.axis_index("tile")
    return t // 4, lax.rem(t // 2, 2), lax.rem(t, 2), lax.axis_index("inner")


def multiply(parts, a_refs, l_all, outs, a_all, result):
    z, _, _, inner = place()
    rows, width = a_refs[0].shape
    for r, ref in enumerate(a_refs):
        a_all[r * rows : (r + 1) * rows, :] = ref[...].astype(a_all.dtype)
    for c in range(width // TILE):
        cols = slice(c * TILE, (c + 1) * TILE)
        result[...] = lax.dot_general(
            a_all[:, cols].astype(jnp.bfloat16),
            l_all[:, cols],
            (((1,), (1,)), ((), ())),
            preferred_element_type=jnp.float32,
        )
        for p in range(len(outs) // 2):
            start = pl.multiple_of((inner ^ p ^ (z // parts)) * rows, rows)
            value = result[pl.ds(start, rows), :]
            outs[2 * p][c] = value
            outs[2 * p + 1][c] = value.astype(jnp.bfloat16)


def first_products_kernel(inner_size, parts, kept, *refs):
    a_refs, l_refs = refs[: inner_size - 1], refs[inner_size - 1 : inner_size + 2]
    outs = refs[inner_size + 2 : 3 * inner_size + 2]
    l_all, a_all, result = refs[3 * inner_size + 2 :]
    _, y, core, _ = place()
    block = l_refs[0].shape[0]
    rows = kept.shape[0] - block
    for q, ref in enumerate((kept.at[rows:, :],) + l_refs):
        where = ((y ^ (q // 2)) * 2 + (core ^ (q % 2))) * block
        l_all[pl.ds(pl.multiple_of(where, block), block), :] = ref[...]
    multiply(parts, (kept.at[:rows, :],) + a_refs, l_all, outs, a_all, result)


def next_products_kernel(inner_size, parts, *refs):
    a_refs, l_all = refs[:inner_size], refs[inner_size]
    outs = refs[inner_size + 1 : 3 * inner_size + 1]
    a_all, result = refs[3 * inner_size + 1 :]
    multiply(parts, a_refs, l_all, outs, a_all, result)


def totals_kernel(inner_size, right_tiles, mask, *refs):
    count = 4 * inner_size
    sources, outs = refs[:count], refs[count:]
    z, y, core, inner = place()
    chip = z * 2 + y
    left_tiles, _, depth = sources[0].shape
    lanes = mask.shape[2]
    for m, out in enumerate(outs):
        first = ((chip ^ m) * 2 + core) * right_tiles
        for d in range(right_tiles):
            for b in range(2):
                blocks = []
                for rel in range(2):
                    total = None
                    for p in range(inner_size):
                        ref = sources[(b * 2 + rel) * inner_size + p]
                        for c in range(left_tiles):
                            on = mask[(inner ^ p) * left_tiles + c, pl.ds(first + d, 1), :]
                            on = jnp.concatenate([on] * (depth // lanes), axis=1)
                            term = on * ref[c].astype(jnp.float32)
                            total = term if total is None else total + term
                    blocks.append(total)
                out[d, b] = jnp.concatenate(blocks, axis=0).astype(jnp.bfloat16)


def residual_kernel(targets, parts, z_half, rows, *refs):
    t_refs = refs[: parts * targets]
    right, occupied, virtual, out = refs[parts * targets :]
    z, y, core, _ = place()
    right_tiles, _, _, depth = t_refs[0].shape
    low = lax.rem(z, parts)
    for d in range(right_tiles):
        cols = slice(d * TILE, (d + 1) * TILE)
        total = None
        for q in range(targets // 2):
            for b in range(2):
                pieces = [
                    t_refs[(o ^ (q % parts)) * targets + 2 * q + rel_y][d, b]
                    for o in range(parts)
                    for rel_y in range(2)
                ]
                start = pl.multiple_of((z ^ q ^ (b * z_half)) * depth, depth)
                term = jnp.dot(
                    jnp.concatenate(pieces, axis=0),
                    right[pl.ds(start, depth), cols],
                    preferred_element_type=jnp.float32,
                )
                total = term if total is None else total + term
        source = 0
        for o in range(parts):
            for rel_y in range(2):
                for rel in range(2):
                    at = (((low ^ o) * 2 + (y ^ rel_y)) * 2 + (core ^ rel)) * rows
                    at = pl.multiple_of(at, rows)
                    shift = occupied[pl.ds(at, rows), :] + virtual[:, cols]
                    out[pl.ds(at, rows), cols] = total[source : source + rows, :] / shift
                    source += rows


def solution(mesh):
    tiles, inner_size = mesh.shape["tile"], mesh.shape["inner"]
    z_size, chips = tiles // 4, tiles // 2
    parts, half, z_half = z_size // inner_size, chips // 2, z_size // 2

    def swap(value, q, axis="tile", size=tiles):
        return lax.ppermute(value, axis, [(t, t ^ q) for t in range(size)])

    def cross(value, p):
        pairs = [
            (t * inner_size + n, (t ^ (4 * z_half)) * inner_size + (n ^ p))
            for t in range(tiles)
            for n in range(inner_size)
        ]
        return lax.ppermute(value, ("tile", "inner"), pairs)

    def call(kernel, operands, in_specs, out_shape, scratch=(), flops=0, moved=1 << 20):
        many = isinstance(out_shape, list)
        return pl.pallas_call(
            kernel,
            out_shape=out_shape,
            in_specs=in_specs,
            out_specs=[VMEM] * len(out_shape) if many else VMEM,
            scratch_shapes=list(scratch),
            compiler_params=PARAMS,
            cost_estimate=cost(flops, moved),
        )(*operands)

    def on_device(amplitudes, left_factors, right_factors, tile_pattern, occupied_shift, virtual_shift):
        rows, width = amplitudes.shape
        block = left_factors.shape[0]
        out_width = right_factors.shape[1]
        left_tiles, right_tiles = width // TILE, out_width // TILE
        depth = 4 * block

        lanes = min(128, depth)
        on = (tile_pattern != 0).astype(jnp.float32)
        mask = jnp.broadcast_to(on[:, :, None], (*tile_pattern.shape, lanes))
        kept = call(
            keep_kernel, (amplitudes, left_factors), [VMEM] * 2, pltpu.VMEM((rows + block, width), amplitudes.dtype)
        )
        by_y = swap(left_factors, 2)
        lefts = [swap(left_factors, 1), by_y, swap(by_y, 1)]
        amps = {q: swap(amplitudes, 4 * q) for q in range(1, z_half + 1)}
        amps |= {q: swap(amps[z_half], 4 * (q ^ z_half)) for q in range(z_half + 1, z_size)}

        packed = jnp.bfloat16 if rows % 16 == 0 else jnp.float32
        scratch = [
            pltpu.VMEM((inner_size * rows, width), packed),
            pltpu.VMEM((inner_size * rows, depth), jnp.float32),
        ]
        shapes = [
            jax.ShapeDtypeStruct((left_tiles, rows, depth), kind)
            for _ in range(inner_size)
            for kind in (jnp.float32, jnp.bfloat16)
        ]
        flops = 2 * inner_size * rows * width * depth
        arrived = []
        for s in range(parts):
            blocks = [amps[r * parts + s] for r in range(inner_size) if r or s]
            if s == 0:
                *products, left_all = call(
                    functools.partial(first_products_kernel, inner_size, parts),
                    (kept, *blocks, *lefts),
                    [VMEM] * (inner_size + 3),
                    shapes + [pltpu.VMEM((depth, width), jnp.bfloat16)],
                    scratch,
                    flops,
                )
            else:
                products = call(
                    functools.partial(next_products_kernel, inner_size, parts),
                    (*blocks, left_all),
                    [VMEM] * (inner_size + 1),
                    shapes,
                    scratch,
                    flops,
                )
            crossed = [cross(products[2 * p + 1], p) for p in range(inner_size)]
            mine = [products[0]]
            mine += [swap(products[2 * p], p, "inner", inner_size) for p in range(1, inner_size)]
            other = [swap(part, 1) for part in mine]
            crossed_other = [swap(part, 1) for part in crossed]
            operands = (mask, *mine, *other, *crossed, *crossed_other)
            made = call(
                functools.partial(totals_kernel, inner_size, right_tiles),
                operands,
                [VMEM] * len(operands),
                [jax.ShapeDtypeStruct((right_tiles, 2, 2 * rows, depth), jnp.bfloat16)] * half,
            )
            arrived += [made[0]] + [swap(made[m], 2 * m) for m in range(1, half)]

        return call(
            functools.partial(residual_kernel, half, parts, z_half, rows),
            (*arrived, right_factors, occupied_shift.reshape(-1, 1), virtual_shift.reshape(1, -1)),
            [VMEM] * (len(arrived) + 3),
            jax.ShapeDtypeStruct((occupied_shift.shape[0], out_width), jnp.float32),
            (),
            2 * occupied_shift.shape[0] * out_width * right_factors.shape[0],
            4 << 20,
        )


    placed = (P("tile", "inner"), P("tile", "inner"), P(None, "tile"), P(), P("inner"), P("tile"))
    return jax.shard_map(on_device, mesh=mesh, in_specs=placed, out_specs=P("inner", "tile"), check_vma=False)
```

profile of v0, /device:TPU:0, one launch (start us, length us, event | category | flops | bytes accessed | tf_op | source)
XLA Modules:
  0.0 61.6 jit_solution(13729975458585212023)
XLA Ops:
  0.0 3.0 %collective-permute-start.2 = (bf16[64,2048]{1,0:T(8,128)(2,1)}, bf16[64,2048]{1,0:T(8,128)(2,1)S(1)}, u32[]{:S(2)}, u32[]{:S(2)}) collective-permute-start(bf16[64,2048]{1,0:T(8,128)(2,1)} %left.1), channel_id=1, source_target_pairs={{0,4},{2,6},{4,0},{6,2},{8,12},{10,14},{12,8},{14,10},{16,20},{18,... | collective-permute-start | bytes 786440 | tf_op jit(solution)/shard_map/ppermute | solution.py:138
  3.0 0.0 collective-permute-start.1
  3.0 6.5 %collective-permute-done.2.refs_2_ = bf16[64,2048]{1,0:T(8,128)(2,1)S(1)} collective-permute-done((bf16[64,2048]{1,0:T(8,128)(2,1)}, bf16[64,2048]{1,0:T(8,128)(2,1)S(1)}, u32[]{:S(2)}, u32[]{:S(2)}) %collective-permute-start.2) | collective-permute-done | bytes 262176 | tf_op jit(solution)/shard_map/ppermute | solution.py:138
  9.5 0.0 collective-permute-start.3
  9.5 2.8 %collective-permute-start = (bf16[32,2048]{1,0:T(8,128)(2,1)}, bf16[32,2048]{1,0:T(8,128)(2,1)S(1)}, u32[]{:S(2)}, u32[]{:S(2)}) collective-permute-start(bf16[32,2048]{1,0:T(8,128)(2,1)} %amplitudes.1), channel_id=1, source_target_pairs={{0,16},{2,18},{4,20},{6,22},{8,24},{10,26},{12,28},{14,30},{16,0},... | collective-permute-start | bytes 393224 | tf_op jit(solution)/shard_map/ppermute | solution.py:138
  12.3 1.6 %collective-permute-start.14 = (bf16[32,2048]{1,0:T(8,128)(2,1)}, bf16[32,2048]{1,0:T(8,128)(2,1)S(1)}, u32[]{:S(2)}, u32[]{:S(2)}) collective-permute-start(bf16[32,2048]{1,0:T(8,128)(2,1)} %amplitudes.1), channel_id=1, source_target_pairs={{0,8},{2,10},{4,12},{6,14},{8,0},{10,2},{12,4},{14,6},{16,24},{18,... | collective-permute-start | bytes 393224 | tf_op jit(solution)/shard_map/ppermute | solution.py:138
  13.9 5.7 %collective-permute-done.refs_0_ = bf16[32,2048]{1,0:T(8,128)(2,1)S(1)} collective-permute-done((bf16[32,2048]{1,0:T(8,128)(2,1)}, bf16[32,2048]{1,0:T(8,128)(2,1)S(1)}, u32[]{:S(2)}, u32[]{:S(2)}) %collective-permute-start) | collective-permute-done | bytes 131104 | tf_op jit(solution)/shard_map/ppermute | solution.py:138
  19.6 0.7 %collective-permute-start.15 = (bf16[32,2048]{1,0:T(8,128)(2,1)S(1)}, bf16[32,2048]{1,0:T(8,128)(2,1)S(1)}, u32[]{:S(2)}, u32[]{:S(2)}) collective-permute-start(bf16[32,2048]{1,0:T(8,128)(2,1)S(1)} %collective-permute-done.refs_0_), channel_id=1, source_target_pairs={{0,8},{2,10},{4,12},{6,14},{8,0},{10,2},{12,4},{14,6},{16,24},{18,... | collective-permute-start | bytes 393224 | tf_op jit(solution)/shard_map/ppermute | solution.py:138
  20.3 0.9 %copy-done.1 = bf16[64,2048]{1,0:T(8,128)(2,1)S(1)} copy-done((bf16[64,2048]{1,0:T(8,128)(2,1)S(1)}, bf16[64,2048]{1,0:T(8,128)(2,1)}, u32[]{:S(2)}) %copy-start.1) | copy-done | bytes 262168
  21.3 0.9 %copy-done.2 = bf16[32,2048]{1,0:T(8,128)(2,1)S(1)} copy-done((bf16[32,2048]{1,0:T(8,128)(2,1)S(1)}, bf16[32,2048]{1,0:T(8,128)(2,1)}, u32[]{:S(2)}) %copy-start.2) | copy-done | bytes 131096
  22.2 0.0 copy-start.5
  22.2 0.0 copy-start
  22.3 0.0 copy-start.3
  22.3 0.0 collective-permute-done.1.refs_1_
  22.3 0.0 collective-permute-done.3.refs_3_
  22.3 0.6 shard_map.65
  22.9 0.0 collective-permute-done.14.refs_0_
  22.9 1.9 %collective-permute-done.15.refs_1_ = bf16[32,2048]{1,0:T(8,128)(2,1)S(1)} collective-permute-done((bf16[32,2048]{1,0:T(8,128)(2,1)S(1)}, bf16[32,2048]{1,0:T(8,128)(2,1)S(1)}, u32[]{:S(2)}, u32[]{:S(2)}) %collective-permute-start.15) | collective-permute-done | bytes 131104 | tf_op jit(solution)/shard_map/ppermute | solution.py:138
  24.7 0.5 shard_map.67
  25.2 2.7 %collective-permute-start.19 = (bf16[4,32,256]{2,1,0:T(8,128)(2,1)S(1)}, bf16[4,32,256]{2,1,0:T(8,128)(2,1)S(1)}, u32[]{:S(2)}, u32[]{:S(2)}) collective-permute-start(bf16[4,32,256]{2,1,0:T(8,128)(2,1)S(1)} %get-tuple-element.33), channel_id=1, source_target_pairs={{0,16},{1,17},{2,18},{3,19},{4,20},{5,21},{6,22},{7,23},{8,24},{9,... | collective-permute-start | bytes 196616 | tf_op jit(solution)/shard_map/ppermute | solution.py:146
  27.9 1.1 %collective-permute-start.20 = (bf16[4,32,256]{2,1,0:T(8,128)(2,1)S(1)}, bf16[4,32,256]{2,1,0:T(8,128)(2,1)S(1)}, u32[]{:S(2)}, u32[]{:S(2)}) collective-permute-start(bf16[4,32,256]{2,1,0:T(8,128)(2,1)S(1)} %get-tuple-element.34), channel_id=1, source_target_pairs={{0,17},{1,16},{2,19},{3,18},{4,21},{5,20},{6,23},{7,22},{8,25},{9,... | collective-permute-start | bytes 196616 | tf_op jit(solution)/shard_map/ppermute | solution.py:146
  29.0 0.6 %collective-permute-start.16 = (f32[4,32,256]{2,1,0:T(8,128)S(1)}, f32[4,32,256]{2,1,0:T(8,128)S(1)}, u32[]{:S(2)}, u32[]{:S(2)}) collective-permute-start(f32[4,32,256]{2,1,0:T(8,128)S(1)} %get-tuple-element.32), channel_id=1, source_target_pairs={{0,1},{1,0},{2,3},{3,2},{4,5},{5,4},{6,7},{7,6},{8,9},{9,8},{10,11... | collective-permute-start | bytes 393224 | tf_op jit(solution)/shard_map/ppermute | solution.py:138
  29.7 0.0 collective-permute-start.17
  29.7 1.4 %collective-permute-start.4 = (f32[4,32,256]{2,1,0:T(8,128)S(1)}, f32[4,32,256]{2,1,0:T(8,128)S(1)}, u32[]{:S(2)}, u32[]{:S(2)}) collective-permute-start(f32[4,32,256]{2,1,0:T(8,128)S(1)} %get-tuple-element.23), channel_id=1, source_target_pairs={{0,1},{1,0},{2,3},{3,2},{4,5},{5,4},{6,7},{7,6},{8,9},{9,8},{10,11... | collective-permute-start | bytes 393224 | tf_op jit(solution)/shard_map/ppermute | solution.py:138
  31.1 0.0 collective-permute-done.19.refs_4_
  31.1 0.2 collective-permute-start.21
  31.3 3.1 %collective-permute-done.20.refs_5_ = bf16[4,32,256]{2,1,0:T(8,128)(2,1)S(1)} collective-permute-done((bf16[4,32,256]{2,1,0:T(8,128)(2,1)S(1)}, bf16[4,32,256]{2,1,0:T(8,128)(2,1)S(1)}, u32[]{:S(2)}, u32[]{:S(2)}) %collective-permute-start.20) | collective-permute-done | bytes 65568 | tf_op jit(solution)/shard_map/ppermute | solution.py:146
  34.4 0.0 collective-permute-start.22
  34.4 0.0 collective-permute-done.21.refs_6_
  34.4 0.8 %collective-permute-start.8 = (bf16[4,32,256]{2,1,0:T(8,128)(2,1)S(1)}, bf16[4,32,256]{2,1,0:T(8,128)(2,1)S(1)}, u32[]{:S(2)}, u32[]{:S(2)}) collective-permute-start(bf16[4,32,256]{2,1,0:T(8,128)(2,1)S(1)} %get-tuple-element.25), channel_id=1, source_target_pairs={{0,17},{1,16},{2,19},{3,18},{4,21},{5,20},{6,23},{7,22},{8,25},{9,... | collective-permute-start | bytes 196616 | tf_op jit(solution)/shard_map/ppermute | solution.py:146
  35.3 0.4 collective-permute-done.22.refs_7_
  35.7 2.3 %collective-permute-start.7 = (bf16[4,32,256]{2,1,0:T(8,128)(2,1)S(1)}, bf16[4,32,256]{2,1,0:T(8,128)(2,1)S(1)}, u32[]{:S(2)}, u32[]{:S(2)}) collective-permute-start(bf16[4,32,256]{2,1,0:T(8,128)(2,1)S(1)} %get-tuple-element.24), channel_id=1, source_target_pairs={{0,16},{1,17},{2,18},{3,19},{4,20},{5,21},{6,22},{7,23},{8,24},{9,... | collective-permute-start | bytes 196616 | tf_op jit(solution)/shard_map/ppermute | solution.py:146
  37.9 0.0 collective-permute-done.16.refs_1_
  37.9 0.0 collective-permute-start.5
  37.9 0.0 collective-permute-done.17.refs_2_
  37.9 0.5 collective-permute-start.18
  38.4 0.0 collective-permute-done.4.refs_1_
  38.4 0.1 collective-permute-start.6
  38.5 0.9 %collective-permute-done.18.refs_3_ = f32[4,32,256]{2,1,0:T(8,128)S(1)} collective-permute-done((f32[4,32,256]{2,1,0:T(8,128)S(1)}, f32[4,32,256]{2,1,0:T(8,128)S(1)}, u32[]{:S(2)}, u32[]{:S(2)}) %collective-permute-start.18) | collective-permute-done | bytes 131104 | tf_op jit(solution)/shard_map/ppermute | solution.py:138
  39.5 0.1 broadcast_in_dim.2.mask
  39.5 0.7 %shard_map.68 = (bf16[2,2,64,256]{3,2,1,0:T(8,128)(2,1)S(1)}, bf16[2,2,64,256]{3,2,1,0:T(8,128)(2,1)S(1)}, bf16[2,2,64,256]{3,2,1,0:T(8,128)(2,1)S(1)}, bf16[2,2,64,256]{3,2,1,0:T(8,128)(2,1)S(1)}) custom-call(f32[8,32,128]{2,1,0:T(8,128)S(1)} %broadcast_in_dim.2.mask, f32[4,32,256]{2,1,0:T(8,128)S(1)} %get-tuple-element.31.refs_0_, ...), custom_call_target="tpu_custom_call" | custom-call | bytes 1048576 | tf_op jit(solution)/shard_map/pallas_call | solution.py:150
  40.3 1.6 %collective-permute-start.23 = (bf16[2,2,64,256]{3,2,1,0:T(8,128)(2,1)S(1)}, bf16[2,2,64,256]{3,2,1,0:T(8,128)(2,1)S(1)}, u32[]{:S(2)}, u32[]{:S(2)}) collective-permute-start(bf16[2,2,64,256]{3,2,1,0:T(8,128)(2,1)S(1)} %get-tuple-element.36), channel_id=1, source_target_pairs={{0,4},{2,6},{4,0},{6,2},{8,12},{10,14},{12,8},{14,10},{16,20},{18,... | collective-permute-start | bytes 393224 | tf_op jit(solution)/shard_map/ppermute | solution.py:138
  41.8 0.7 %collective-permute-done.8.refs_5_ = bf16[4,32,256]{2,1,0:T(8,128)(2,1)S(1)} collective-permute-done((bf16[4,32,256]{2,1,0:T(8,128)(2,1)S(1)}, bf16[4,32,256]{2,1,0:T(8,128)(2,1)S(1)}, u32[]{:S(2)}, u32[]{:S(2)}) %collective-permute-start.8) | collective-permute-done | bytes 65568 | tf_op jit(solution)/shard_map/ppermute | solution.py:146
  42.6 0.0 collective-permute-start.10
  42.6 2.0 %collective-permute-done.7.refs_4_ = bf16[4,32,256]{2,1,0:T(8,128)(2,1)S(1)} collective-permute-done((bf16[4,32,256]{2,1,0:T(8,128)(2,1)S(1)}, bf16[4,32,256]{2,1,0:T(8,128)(2,1)S(1)}, u32[]{:S(2)}, u32[]{:S(2)}) %collective-permute-start.7) | collective-permute-done | bytes 65568 | tf_op jit(solution)/shard_map/ppermute | solution.py:146
  44.6 0.0 collective-permute-start.9
  44.6 0.0 collective-permute-done.10.refs_7_
  44.6 0.8 %collective-permute-start.24 = (bf16[2,2,64,256]{3,2,1,0:T(8,128)(2,1)S(1)}, bf16[2,2,64,256]{3,2,1,0:T(8,128)(2,1)S(1)}, u32[]{:S(2)}, u32[]{:S(2)}) collective-permute-start(bf16[2,2,64,256]{3,2,1,0:T(8,128)(2,1)S(1)} %get-tuple-element.37), channel_id=1, source_target_pairs={{0,8},{2,10},{4,12},{6,14},{8,0},{10,2},{12,4},{14,6},{16,24},{18,... | collective-permute-start | bytes 393224 | tf_op jit(solution)/shard_map/ppermute | solution.py:138
  45.4 0.4 collective-permute-done.9.refs_6_
  45.9 1.7 %collective-permute-start.25 = (bf16[2,2,64,256]{3,2,1,0:T(8,128)(2,1)S(1)}, bf16[2,2,64,256]{3,2,1,0:T(8,128)(2,1)S(1)}, u32[]{:S(2)}, u32[]{:S(2)}) collective-permute-start(bf16[2,2,64,256]{3,2,1,0:T(8,128)(2,1)S(1)} %get-tuple-element.38), channel_id=1, source_target_pairs={{0,12},{2,14},{4,8},{6,10},{8,4},{10,6},{12,0},{14,2},{16,28},{18,... | collective-permute-start | bytes 393224 | tf_op jit(solution)/shard_map/ppermute | solution.py:138
  47.6 0.0 collective-permute-done.5.refs_2_
  47.6 0.0 collective-permute-done.6.refs_3_
  47.6 1.2 %shard_map.66 = (bf16[2,2,64,256]{3,2,1,0:T(8,128)(2,1)S(1)}, bf16[2,2,64,256]{3,2,1,0:T(8,128)(2,1)}, bf16[2,2,64,256]{3,2,1,0:T(8,128)(2,1)}, bf16[2,2,64,256]{3,2,1,0:T(8,128)(2,1)}) custom-call(f32[8,32,128]{2,1,0:T(8,128)S(1)} %broadcast_in_dim.2.mask, f32[4,32,256]{2,1,0:T(8,128)S(1)} %get-tuple-element.22.refs_0_, ...), custom_call_target="tpu_custom_call" | custom-call | bytes 1048576 | tf_op jit(solution)/shard_map/pallas_call | solution.py:150
  48.8 0.5 collective-permute-start.11
  49.3 1.2 %collective-permute-start.12 = (bf16[2,2,64,256]{3,2,1,0:T(8,128)(2,1)}, bf16[2,2,64,256]{3,2,1,0:T(8,128)(2,1)S(1)}, u32[]{:S(2)}, u32[]{:S(2)}) collective-permute-start(bf16[2,2,64,256]{3,2,1,0:T(8,128)(2,1)} %get-tuple-element.28), channel_id=1, source_target_pairs={{0,8},{2,10},{4,12},{6,14},{8,0},{10,2},{12,4},{14,6},{16,24},{18,... | collective-permute-start | bytes 393224 | tf_op jit(solution)/shard_map/ppermute | solution.py:138
  50.5 0.0 collective-permute-done.23.refs_5_
  50.5 1.7 %collective-permute-start.13 = (bf16[2,2,64,256]{3,2,1,0:T(8,128)(2,1)}, bf16[2,2,64,256]{3,2,1,0:T(8,128)(2,1)S(1)}, u32[]{:S(2)}, u32[]{:S(2)}) collective-permute-start(bf16[2,2,64,256]{3,2,1,0:T(8,128)(2,1)} %get-tuple-element.29), channel_id=1, source_target_pairs={{0,12},{2,14},{4,8},{6,10},{8,4},{10,6},{12,0},{14,2},{16,28},{18,... | collective-permute-start | bytes 393224 | tf_op jit(solution)/shard_map/ppermute | solution.py:138
  52.3 0.1 copy.7.refs_9_
  52.4 0.0 collective-permute-done.24.refs_6_
  52.4 2.3 %collective-permute-done.25.refs_7_ = bf16[2,2,64,256]{3,2,1,0:T(8,128)(2,1)S(1)} collective-permute-done((bf16[2,2,64,256]{3,2,1,0:T(8,128)(2,1)S(1)}, bf16[2,2,64,256]{3,2,1,0:T(8,128)(2,1)S(1)}, u32[]{:S(2)}, u32[]{:S(2)}) %collective-permute-start.25) | collective-permute-done | bytes 131104 | tf_op jit(solution)/shard_map/ppermute | solution.py:138
  54.8 2.3 %collective-permute-done.11.refs_1_ = bf16[2,2,64,256]{3,2,1,0:T(8,128)(2,1)S(1)} collective-permute-done((bf16[2,2,64,256]{3,2,1,0:T(8,128)(2,1)}, bf16[2,2,64,256]{3,2,1,0:T(8,128)(2,1)S(1)}, u32[]{:S(2)}, u32[]{:S(2)}) %collective-permute-start.11) | collective-permute-done | bytes 131104 | tf_op jit(solution)/shard_map/ppermute | solution.py:138
  57.1 0.0 collective-permute-done.12.refs_2_
  57.1 2.8 %collective-permute-done.13.refs_3_ = bf16[2,2,64,256]{3,2,1,0:T(8,128)(2,1)S(1)} collective-permute-done((bf16[2,2,64,256]{3,2,1,0:T(8,128)(2,1)}, bf16[2,2,64,256]{3,2,1,0:T(8,128)(2,1)S(1)}, u32[]{:S(2)}, u32[]{:S(2)}) %collective-permute-start.13) | collective-permute-done | bytes 131104 | tf_op jit(solution)/shard_map/ppermute | solution.py:138
  59.9 1.7 %shard_map.69 = f32[256,1024]{1,0:T(8,128)} custom-call(bf16[2,2,64,256]{3,2,1,0:T(8,128)(2,1)S(1)} %get-tuple-element.26.refs_0_, bf16[2,2,64,256]{3,2,1,0:T(8,128)(2,1)S(1)} %collective-permute-done.11.refs_1_, bf16[2,2,64,256]{3,2,1,0:T(8,128)(2,1)S(1)} %collective-permute-done.12.refs_2_, bf16[2,2,64,256]{3,2,1,0:T(8,128)(2,1)S(1)} %collective-permute-done.13.refs_3_, ...), custom_call_target="tpu_custom_call" | custom-call | flops 536870912 | bytes 4194304 | tf_op jit(solution)/shard_map/pallas_call | solution.py:150
  (9 shorter events, 0.0 us)
Async XLA Ops:
  0.0 9.5 %collective-permute-start.2 = (bf16[64,2048]{1,0:T(8,128)(2,1)}, bf16[64,2048]{1,0:T(8,128)(2,1)S(1)}, u32[]{:S(2)}, u32[]{:S(2)}) collective-permute-start(bf16[64,2048]{1,0:T(8,128)(2,1)} %left.1), channel_id=1, source_target_pairs={{0,4},{2,6},{4,0},{6,2},{8,12},{10,14},{12,8},{14,10},{16,20},{18,... | collective-permute-start | bytes 786440 | tf_op jit(solution)/shard_map/ppermute | solution.py:138
  3.0 19.3 %collective-permute-start.1 = (bf16[64,2048]{1,0:T(8,128)(2,1)}, bf16[64,2048]{1,0:T(8,128)(2,1)S(1)}, u32[]{:S(2)}, u32[]{:S(2)}) collective-permute-start(bf16[64,2048]{1,0:T(8,128)(2,1)} %left.1), channel_id=1, source_target_pairs={{0,2},{2,0},{4,6},{6,4},{8,10},{10,8},{12,14},{14,12},{16,18},{18,... | collective-permute-start | bytes 786440 | tf_op jit(solution)/shard_map/ppermute | solution.py:138
  9.5 12.8 %collective-permute-start.3 = (bf16[64,2048]{1,0:T(8,128)(2,1)S(1)}, bf16[64,2048]{1,0:T(8,128)(2,1)S(1)}, u32[]{:S(2)}, u32[]{:S(2)}) collective-permute-start(bf16[64,2048]{1,0:T(8,128)(2,1)S(1)} %collective-permute-done.2.refs_2_), channel_id=1, source_target_pairs={{0,2},{2,0},{4,6},{6,4},{8,10},{10,8},{12,14},{14,12},{16,18},{18,... | collective-permute-start | bytes 786440 | tf_op jit(solution)/shard_map/ppermute | solution.py:138
  9.5 10.1 %collective-permute-start = (bf16[32,2048]{1,0:T(8,128)(2,1)}, bf16[32,2048]{1,0:T(8,128)(2,1)S(1)}, u32[]{:S(2)}, u32[]{:S(2)}) collective-permute-start(bf16[32,2048]{1,0:T(8,128)(2,1)} %amplitudes.1), channel_id=1, source_target_pairs={{0,16},{2,18},{4,20},{6,22},{8,24},{10,26},{12,28},{14,30},{16,0},... | collective-permute-start | bytes 393224 | tf_op jit(solution)/shard_map/ppermute | solution.py:138
  12.3 10.5 %collective-permute-start.14 = (bf16[32,2048]{1,0:T(8,128)(2,1)}, bf16[32,2048]{1,0:T(8,128)(2,1)S(1)}, u32[]{:S(2)}, u32[]{:S(2)}) collective-permute-start(bf16[32,2048]{1,0:T(8,128)(2,1)} %amplitudes.1), channel_id=1, source_target_pairs={{0,8},{2,10},{4,12},{6,14},{8,0},{10,2},{12,4},{14,6},{16,24},{18,... | collective-permute-start | bytes 393224 | tf_op jit(solution)/shard_map/ppermute | solution.py:138
  19.6 5.1 %collective-permute-start.15 = (bf16[32,2048]{1,0:T(8,128)(2,1)S(1)}, bf16[32,2048]{1,0:T(8,128)(2,1)S(1)}, u32[]{:S(2)}, u32[]{:S(2)}) collective-permute-start(bf16[32,2048]{1,0:T(8,128)(2,1)S(1)} %collective-permute-done.refs_0_), channel_id=1, source_target_pairs={{0,8},{2,10},{4,12},{6,14},{8,0},{10,2},{12,4},{14,6},{16,24},{18,... | collective-permute-start | bytes 393224 | tf_op jit(solution)/shard_map/ppermute | solution.py:138
  20.3 0.9 %copy-start.1 = (bf16[64,2048]{1,0:T(8,128)(2,1)S(1)}, bf16[64,2048]{1,0:T(8,128)(2,1)}, u32[]{:S(2)}) copy-start(bf16[64,2048]{1,0:T(8,128)(2,1)} %left.1) | copy-start | bytes 786436
  21.3 0.9 %copy-start.2 = (bf16[32,2048]{1,0:T(8,128)(2,1)S(1)}, bf16[32,2048]{1,0:T(8,128)(2,1)}, u32[]{:S(2)}) copy-start(bf16[32,2048]{1,0:T(8,128)(2,1)} %amplitudes.1) | copy-start | bytes 393220
  22.2 16.3 %copy-start.4 = (s32[8,32]{1,0:T(8,128)S(1)}, s32[8,32]{1,0:T(8,128)}, u32[]{:S(2)}) copy-start(s32[8,32]{1,0:T(8,128)} %param.9) | copy-start | bytes 3076
  22.2 30.1 %copy-start.5 = (f32[256]{0:T(256)S(1)}, f32[256]{0:T(256)}, u32[]{:S(2)}) copy-start(f32[256]{0:T(256)} %param.10) | copy-start | bytes 3076
  22.2 37.7 %copy-start = (bf16[1024,1024]{1,0:T(8,128)(2,1)S(1)}, bf16[1024,1024]{1,0:T(8,128)(2,1)}, u32[]{:S(2)}) copy-start(bf16[1024,1024]{1,0:T(8,128)(2,1)} %refs_8_.1) | copy-start | bytes 6291460
  22.3 37.7 %copy-start.3 = (f32[1024]{0:T(1024)S(1)}, f32[1024]{0:T(1024)}, u32[]{:S(2)}) copy-start(f32[1024]{0:T(1024)} %param.11) | copy-start | bytes 12292
  25.2 5.9 %collective-permute-start.19 = (bf16[4,32,256]{2,1,0:T(8,128)(2,1)S(1)}, bf16[4,32,256]{2,1,0:T(8,128)(2,1)S(1)}, u32[]{:S(2)}, u32[]{:S(2)}) collective-permute-start(bf16[4,32,256]{2,1,0:T(8,128)(2,1)S(1)} %get-tuple-element.33), channel_id=1, source_target_pairs={{0,16},{1,17},{2,18},{3,19},{4,20},{5,21},{6,22},{7,23},{8,24},{9,... | collective-permute-start | bytes 196616 | tf_op jit(solution)/shard_map/ppermute | solution.py:146
  27.9 6.5 %collective-permute-start.20 = (bf16[4,32,256]{2,1,0:T(8,128)(2,1)S(1)}, bf16[4,32,256]{2,1,0:T(8,128)(2,1)S(1)}, u32[]{:S(2)}, u32[]{:S(2)}) collective-permute-start(bf16[4,32,256]{2,1,0:T(8,128)(2,1)S(1)} %get-tuple-element.34), channel_id=1, source_target_pairs={{0,17},{1,16},{2,19},{3,18},{4,21},{5,20},{6,23},{7,22},{8,25},{9,... | collective-permute-start | bytes 196616 | tf_op jit(solution)/shard_map/ppermute | solution.py:146
  29.0 8.9 %collective-permute-start.16 = (f32[4,32,256]{2,1,0:T(8,128)S(1)}, f32[4,32,256]{2,1,0:T(8,128)S(1)}, u32[]{:S(2)}, u32[]{:S(2)}) collective-permute-start(f32[4,32,256]{2,1,0:T(8,128)S(1)} %get-tuple-element.32), channel_id=1, source_target_pairs={{0,1},{1,0},{2,3},{3,2},{4,5},{5,4},{6,7},{7,6},{8,9},{9,8},{10,11... | collective-permute-start | bytes 393224 | tf_op jit(solution)/shard_map/ppermute | solution.py:138
  29.7 8.3 %collective-permute-start.17 = (f32[4,32,256]{2,1,0:T(8,128)S(1)}, f32[4,32,256]{2,1,0:T(8,128)S(1)}, u32[]{:S(2)}, u32[]{:S(2)}) collective-permute-start(f32[4,32,256]{2,1,0:T(8,128)S(1)} %get-tuple-element.31.refs_0_), channel_id=1, source_target_pairs={{0,2},{2,0},{4,6},{6,4},{8,10},{10,8},{12,14},{14,12},{16,18},{18,... | collective-permute-start | bytes 393224 | tf_op jit(solution)/shard_map/ppermute | solution.py:138
  29.7 8.8 %collective-permute-start.4 = (f32[4,32,256]{2,1,0:T(8,128)S(1)}, f32[4,32,256]{2,1,0:T(8,128)S(1)}, u32[]{:S(2)}, u32[]{:S(2)}) collective-permute-start(f32[4,32,256]{2,1,0:T(8,128)S(1)} %get-tuple-element.23), channel_id=1, source_target_pairs={{0,1},{1,0},{2,3},{3,2},{4,5},{5,4},{6,7},{7,6},{8,9},{9,8},{10,11... | collective-permute-start | bytes 393224 | tf_op jit(solution)/shard_map/ppermute | solution.py:138
  31.1 3.4 %collective-permute-start.21 = (bf16[4,32,256]{2,1,0:T(8,128)(2,1)S(1)}, bf16[4,32,256]{2,1,0:T(8,128)(2,1)S(1)}, u32[]{:S(2)}, u32[]{:S(2)}) collective-permute-start(bf16[4,32,256]{2,1,0:T(8,128)(2,1)S(1)} %collective-permute-done.19.refs_4_), channel_id=1, source_target_pairs={{0,2},{2,0},{4,6},{6,4},{8,10},{10,8},{12,14},{14,12},{16,18},{18,... | collective-permute-start | bytes 196616 | tf_op jit(solution)/shard_map/ppermute | solution.py:138
  34.4 1.3 %collective-permute-start.22 = (bf16[4,32,256]{2,1,0:T(8,128)(2,1)S(1)}, bf16[4,32,256]{2,1,0:T(8,128)(2,1)S(1)}, u32[]{:S(2)}, u32[]{:S(2)}) collective-permute-start(bf16[4,32,256]{2,1,0:T(8,128)(2,1)S(1)} %collective-permute-done.20.refs_5_), channel_id=1, source_target_pairs={{0,2},{2,0},{4,6},{6,4},{8,10},{10,8},{12,14},{14,12},{16,18},{18,... | collective-permute-start | bytes 196616 | tf_op jit(solution)/shard_map/ppermute | solution.py:138
  34.4 8.2 %collective-permute-start.8 = (bf16[4,32,256]{2,1,0:T(8,128)(2,1)S(1)}, bf16[4,32,256]{2,1,0:T(8,128)(2,1)S(1)}, u32[]{:S(2)}, u32[]{:S(2)}) collective-permute-start(bf16[4,32,256]{2,1,0:T(8,128)(2,1)S(1)} %get-tuple-element.25), channel_id=1, source_target_pairs={{0,17},{1,16},{2,19},{3,18},{4,21},{5,20},{6,23},{7,22},{8,25},{9,... | collective-permute-start | bytes 196616 | tf_op jit(solution)/shard_map/ppermute | solution.py:146
  35.7 8.9 %collective-permute-start.7 = (bf16[4,32,256]{2,1,0:T(8,128)(2,1)S(1)}, bf16[4,32,256]{2,1,0:T(8,128)(2,1)S(1)}, u32[]{:S(2)}, u32[]{:S(2)}) collective-permute-start(bf16[4,32,256]{2,1,0:T(8,128)(2,1)S(1)} %get-tuple-element.24), channel_id=1, source_target_pairs={{0,16},{1,17},{2,18},{3,19},{4,20},{5,21},{6,22},{7,23},{8,24},{9,... | collective-permute-start | bytes 196616 | tf_op jit(solution)/shard_map/ppermute | solution.py:146
  37.9 9.7 %collective-permute-start.5 = (f32[4,32,256]{2,1,0:T(8,128)S(1)}, f32[4,32,256]{2,1,0:T(8,128)S(1)}, u32[]{:S(2)}, u32[]{:S(2)}) collective-permute-start(f32[4,32,256]{2,1,0:T(8,128)S(1)} %get-tuple-element.22.refs_0_), channel_id=1, source_target_pairs={{0,2},{2,0},{4,6},{6,4},{8,10},{10,8},{12,14},{14,12},{16,18},{18,... | collective-permute-start | bytes 393224 | tf_op jit(solution)/shard_map/ppermute | solution.py:138
  37.9 1.5 %collective-permute-start.18 = (f32[4,32,256]{2,1,0:T(8,128)S(1)}, f32[4,32,256]{2,1,0:T(8,128)S(1)}, u32[]{:S(2)}, u32[]{:S(2)}) collective-permute-start(f32[4,32,256]{2,1,0:T(8,128)S(1)} %collective-permute-done.16.refs_1_), channel_id=1, source_target_pairs={{0,2},{2,0},{4,6},{6,4},{8,10},{10,8},{12,14},{14,12},{16,18},{18,... | collective-permute-start | bytes 393224 | tf_op jit(solution)/shard_map/ppermute | solution.py:138
  38.4 9.2 %collective-permute-start.6 = (f32[4,32,256]{2,1,0:T(8,128)S(1)}, f32[4,32,256]{2,1,0:T(8,128)S(1)}, u32[]{:S(2)}, u32[]{:S(2)}) collective-permute-start(f32[4,32,256]{2,1,0:T(8,128)S(1)} %collective-permute-done.4.refs_1_), channel_id=1, source_target_pairs={{0,2},{2,0},{4,6},{6,4},{8,10},{10,8},{12,14},{14,12},{16,18},{18,... | collective-permute-start | bytes 393224 | tf_op jit(solution)/shard_map/ppermute | solution.py:138
  40.3 10.3 %collective-permute-start.23 = (bf16[2,2,64,256]{3,2,1,0:T(8,128)(2,1)S(1)}, bf16[2,2,64,256]{3,2,1,0:T(8,128)(2,1)S(1)}, u32[]{:S(2)}, u32[]{:S(2)}) collective-permute-start(bf16[2,2,64,256]{3,2,1,0:T(8,128)(2,1)S(1)} %get-tuple-element.36), channel_id=1, source_target_pairs={{0,4},{2,6},{4,0},{6,2},{8,12},{10,14},{12,8},{14,10},{16,20},{18,... | collective-permute-start | bytes 393224 | tf_op jit(solution)/shard_map/ppermute | solution.py:138
  42.6 2.0 %collective-permute-start.10 = (bf16[4,32,256]{2,1,0:T(8,128)(2,1)S(1)}, bf16[4,32,256]{2,1,0:T(8,128)(2,1)S(1)}, u32[]{:S(2)}, u32[]{:S(2)}) collective-permute-start(bf16[4,32,256]{2,1,0:T(8,128)(2,1)S(1)} %collective-permute-done.8.refs_5_), channel_id=1, source_target_pairs={{0,2},{2,0},{4,6},{6,4},{8,10},{10,8},{12,14},{14,12},{16,18},{18,... | collective-permute-start | bytes 196616 | tf_op jit(solution)/shard_map/ppermute | solution.py:138
  44.6 1.3 %collective-permute-start.9 = (bf16[4,32,256]{2,1,0:T(8,128)(2,1)S(1)}, bf16[4,32,256]{2,1,0:T(8,128)(2,1)S(1)}, u32[]{:S(2)}, u32[]{:S(2)}) collective-permute-start(bf16[4,32,256]{2,1,0:T(8,128)(2,1)S(1)} %collective-permute-done.7.refs_4_), channel_id=1, source_target_pairs={{0,2},{2,0},{4,6},{6,4},{8,10},{10,8},{12,14},{14,12},{16,18},{18,... | collective-permute-start | bytes 196616 | tf_op jit(solution)/shard_map/ppermute | solution.py:138
  44.6 7.8 %collective-permute-start.24 = (bf16[2,2,64,256]{3,2,1,0:T(8,128)(2,1)S(1)}, bf16[2,2,64,256]{3,2,1,0:T(8,128)(2,1)S(1)}, u32[]{:S(2)}, u32[]{:S(2)}) collective-permute-start(bf16[2,2,64,256]{3,2,1,0:T(8,128)(2,1)S(1)} %get-tuple-element.37), channel_id=1, source_target_pairs={{0,8},{2,10},{4,12},{6,14},{8,0},{10,2},{12,4},{14,6},{16,24},{18,... | collective-permute-start | bytes 393224 | tf_op jit(solution)/shard_map/ppermute | solution.py:138
  45.9 8.9 %collective-permute-start.25 = (bf16[2,2,64,256]{3,2,1,0:T(8,128)(2,1)S(1)}, bf16[2,2,64,256]{3,2,1,0:T(8,128)(2,1)S(1)}, u32[]{:S(2)}, u32[]{:S(2)}) collective-permute-start(bf16[2,2,64,256]{3,2,1,0:T(8,128)(2,1)S(1)} %get-tuple-element.38), channel_id=1, source_target_pairs={{0,12},{2,14},{4,8},{6,10},{8,4},{10,6},{12,0},{14,2},{16,28},{18,... | collective-permute-start | bytes 393224 | tf_op jit(solution)/shard_map/ppermute | solution.py:138
  48.8 8.3 %collective-permute-start.11 = (bf16[2,2,64,256]{3,2,1,0:T(8,128)(2,1)}, bf16[2,2,64,256]{3,2,1,0:T(8,128)(2,1)S(1)}, u32[]{:S(2)}, u32[]{:S(2)}) collective-permute-start(bf16[2,2,64,256]{3,2,1,0:T(8,128)(2,1)} %get-tuple-element.27), channel_id=1, source_target_pairs={{0,4},{2,6},{4,0},{6,2},{8,12},{10,14},{12,8},{14,10},{16,20},{18,... | collective-permute-start | bytes 393224 | tf_op jit(solution)/shard_map/ppermute | solution.py:138
  49.3 7.8 %collective-permute-start.12 = (bf16[2,2,64,256]{3,2,1,0:T(8,128)(2,1)}, bf16[2,2,64,256]{3,2,1,0:T(8,128)(2,1)S(1)}, u32[]{:S(2)}, u32[]{:S(2)}) collective-permute-start(bf16[2,2,64,256]{3,2,1,0:T(8,128)(2,1)} %get-tuple-element.28), channel_id=1, source_target_pairs={{0,8},{2,10},{4,12},{6,14},{8,0},{10,2},{12,4},{14,6},{16,24},{18,... | collective-permute-start | bytes 393224 | tf_op jit(solution)/shard_map/ppermute | solution.py:138
  50.5 9.4 %collective-permute-start.13 = (bf16[2,2,64,256]{3,2,1,0:T(8,128)(2,1)}, bf16[2,2,64,256]{3,2,1,0:T(8,128)(2,1)S(1)}, u32[]{:S(2)}, u32[]{:S(2)}) collective-permute-start(bf16[2,2,64,256]{3,2,1,0:T(8,128)(2,1)} %get-tuple-element.29), channel_id=1, source_target_pairs={{0,12},{2,14},{4,8},{6,10},{8,4},{10,6},{12,0},{14,2},{16,28},{18,... | collective-permute-start | bytes 393224 | tf_op jit(solution)/shard_map/ppermute | solution.py:138
where the time goes:
time: 61.8 us; the launch traced here: 61.6 us
  waiting for transfers between devices  29.3 us (47%)
  starting transfers between devices  25.5 us (41%)
  Pallas kernels  4.64 us (8%)
  local copies, waits for them, and re-layouts  2.09 us (3%)
    ppermute x22, waiting for transfers between devices, swap(): return lax.ppermute(value, axis, [(t, t ^ q) for t in range(size)])  23.4 us
    ppermute x22, starting transfers between devices, swap(): return lax.ppermute(value, axis, [(t, t ^ q) for t in range(size)])  18.6 us
    ppermute x4, starting transfers between devices, cross(): return lax.ppermute(value, ('tile', 'inner'), pairs)  6.92 us
    ppermute x4, waiting for transfers between devices, cross(): return lax.ppermute(value, ('tile', 'inner'), pairs)  5.88 us
    pallas_call x6, Pallas kernels, call(): pl.pallas_call(kernel, out_shape=out_shape, in_specs=in_specs, out_specs=...  4.64 us
    unnamed x12, local copies, waits for them, and re-layouts  1.88 us
  transfers between devices with their start and end apart: 26, of which 12 were waited for; matrix products, arithmetic and copies ran while one was open for 0% of the time, Pallas kernels for 4%

commit v1 on v0

--- a/solution.py
+++ b/solution.py
@@ -70,34 +70,62 @@
     multiply(parts, a_refs, l_all, outs, a_all, result)
 
 
-def totals_kernel(inner_size, right_tiles, mask, *refs):
+def weights_kernel(inner_size, left_tiles, right_tiles, targets, rows, mask, out):
+    z, y, core, inner = place()
+    chip = z * 2 + y
+    count = inner_size * left_tiles
+    lanes = mask.shape[2]
+    lane = lax.broadcasted_iota(jnp.int32, (rows, count * rows), 1)
+    diagonal = lax.rem(lane, rows) == lax.broadcasted_iota(jnp.int32, (rows, count * rows), 0)
+    block = lane // rows
+    for m in range(targets):
+        for d in range(right_tiles):
+            column = ((chip ^ m) * 2 + core) * right_tiles + d
+            value = jnp.zeros((rows, count * rows), jnp.float32)
+            for i in range(count):
+                row = (inner ^ (i // left_tiles)) * left_tiles + i % left_tiles
+                on = mask[row, pl.ds(column, 1), :]
+                value = jnp.where(block == i, jnp.concatenate([on] * (count * rows // lanes), axis=1), value)
+            at = (m * right_tiles + d) * rows
+            out[at : at + rows, :] = jnp.where(diagonal, value, 0.0).astype(jnp.bfloat16)
+
+
+def totals_kernel(inner_size, right_tiles, weights, *refs):
     count = 4 * inner_size
     sources, outs = refs[:count], refs[count:]
-    z, y, core, inner = place()
-    chip = z * 2 + y
-    left_tiles, _, depth = sources[0].shape
-    lanes = mask.shape[2]
-    for m, out in enumerate(outs):
-        first = ((chip ^ m) * 2 + core) * right_tiles
-        for d in range(right_tiles):
-            for b in range(2):
-                blocks = []
-                for rel in range(2):
-                    total = None
-                    for p in range(inner_size):
-                        ref = sources[(b * 2 + rel) * inner_size + p]
-                        for c in range(left_tiles):
-                            on = mask[(inner ^ p) * left_tiles + c, pl.ds(first + d, 1), :]
-                            on = jnp.concatenate([on] * (depth // lanes), axis=1)
-                            term = on * ref[c].astype(jnp.float32)
-                            total = term if total is None else total + term
-                    blocks.append(total)
-                out[d, b] = jnp.concatenate(blocks, axis=0).astype(jnp.bfloat16)
+    left_tiles, rows, depth = sources[0].shape
+    shape = (left_tiles * rows, depth)
+    for b in range(2):
+        for rel in range(2):
+            high, low = [], []
+            for p in range(inner_size):
+                ref = sources[(b * 2 + rel) * inner_size + p]
+                value = ref[...]
+                if ref.dtype == jnp.float32 or rows % 16:
+                    value = value.astype(jnp.float32).reshape(shape)
+                    rounded = value.astype(jnp.bfloat16)
+                    low.append((value - rounded.astype(jnp.float32)).astype(jnp.bfloat16))
+                    value = rounded
+                high.append(value.reshape(shape))
+            total = jnp.dot(weights[...], jnp.concatenate(high, axis=0), preferred_element_type=jnp.float32)
+            if b == 0:
+                total += jnp.dot(weights[...], jnp.concatenate(low, axis=0), preferred_element_type=jnp.float32)
+            for m, out in enumerate(outs):
+                for d in range(right_tiles):
+                    at = (m * right_tiles + d) * rows
+                    out[d, b, rel * rows : (rel + 1) * rows, :] = total[at : at + rows, :].astype(jnp.bfloat16)
+
+
+def inverse_kernel(occupied, virtual, out):
+    lanes = 128
+    column = jnp.broadcast_to(occupied[...], (lanes, out.shape[0])).T
+    for at in range(0, out.shape[1], lanes):
+        out[:, at : at + lanes] = 1.0 / (column + virtual[:, at : at + lanes])
 
 
 def residual_kernel(targets, parts, z_half, rows, *refs):
     t_refs = refs[: parts * targets]
-    right, occupied, virtual, out = refs[parts * targets :]
+    right, inverse, out, staged, left, sem = refs[parts * targets :]
     z, y, core, _ = place()
     right_tiles, _, _, depth = t_refs[0].shape
     low = lax.rem(z, parts)
@@ -111,22 +139,29 @@
                     for o in range(parts)
                     for rel_y in range(2)
                 ]
-                start = pl.multiple_of((z ^ q ^ (b * z_half)) * depth, depth)
-                term = jnp.dot(
-                    jnp.concatenate(pieces, axis=0),
-                    right[pl.ds(start, depth), cols],
-                    preferred_element_type=jnp.float32,
-                )
-                total = term if total is None else total + term
+                at = pl.ds(pl.multiple_of((z ^ q ^ (b * z_half)) * depth, depth), depth)
+                if depth % 128 == 0:
+                    for i, piece in enumerate(pieces):
+                        left[d, i * 2 * rows : (i + 1) * 2 * rows, at] = piece
+                else:
+                    piece = jnp.concatenate(pieces, axis=0)
+                    term = jnp.dot(piece, right[at, cols], preferred_element_type=jnp.float32)
+                    total = term if total is None else total + term
+        if depth % 128 == 0:
+            total = jnp.dot(left[d], right[:, cols], preferred_element_type=jnp.float32)
         source = 0
         for o in range(parts):
             for rel_y in range(2):
                 for rel in range(2):
                     at = (((low ^ o) * 2 + (y ^ rel_y)) * 2 + (core ^ rel)) * rows
                     at = pl.multiple_of(at, rows)
-                    shift = occupied[pl.ds(at, rows), :] + virtual[:, cols]
-                    out[pl.ds(at, rows), cols] = total[source : source + rows, :] / shift
+                    scale = inverse[pl.ds(at, rows), cols]
+                    staged[pl.ds(at, rows), cols] = total[source : source + rows, :] * scale
                     source += rows
+        pltpu.make_async_copy(staged.at[:, cols], out.at[:, cols], sem.at[d]).start()
+    for d in range(right_tiles):
+        cols = slice(d * TILE, (d + 1) * TILE)
+        pltpu.make_async_copy(staged.at[:, cols], out.at[:, cols], sem.at[d]).wait()
 
 
 def solution(mesh):
@@ -145,13 +180,13 @@
         ]
         return lax.ppermute(value, ("tile", "inner"), pairs)
 
-    def call(kernel, operands, in_specs, out_shape, scratch=(), flops=0, moved=1 << 20):
+    def call(name, kernel, operands, in_specs, out_shape, scratch=(), flops=0, moved=1 << 20):
         many = isinstance(out_shape, list)
         return pl.pallas_call(
             kernel,
             out_shape=out_shape,
             in_specs=in_specs,
-            out_specs=[VMEM] * len(out_shape) if many else VMEM,
+            out_specs=[VMEM] * len(out_shape) if many else ANY if name == "residual" else VMEM,
             scratch_shapes=list(scratch),
             compiler_params=PARAMS,
             cost_estimate=cost(flops, moved),
@@ -167,8 +202,19 @@
         lanes = min(128, depth)
         on = (tile_pattern != 0).astype(jnp.float32)
         mask = jnp.broadcast_to(on[:, :, None], (*tile_pattern.shape, lanes))
+        weights = call(
+            "weights",
+            functools.partial(weights_kernel, inner_size, left_tiles, right_tiles, half, rows),
+            (mask,),
+            [VMEM],
+            pltpu.VMEM((half * right_tiles * rows, inner_size * left_tiles * rows), jnp.bfloat16),
+        )
         kept = call(
-            keep_kernel, (amplitudes, left_factors), [VMEM] * 2, pltpu.VMEM((rows + block, width), amplitudes.dtype)
+            "keep",
+            keep_kernel,
+            (amplitudes, left_factors),
+            [VMEM] * 2,
+            pltpu.VMEM((rows + block, width), amplitudes.dtype),
         )
         by_y = swap(left_factors, 2)
         lefts = [swap(left_factors, 1), by_y, swap(by_y, 1)]
@@ -181,7 +227,7 @@
             pltpu.VMEM((inner_size * rows, depth), jnp.float32),
         ]
         shapes = [
-            jax.ShapeDtypeStruct((left_tiles, rows, depth), kind)
+            pltpu.VMEM((left_tiles, rows, depth), kind)
             for _ in range(inner_size)
             for kind in (jnp.float32, jnp.bfloat16)
         ]
@@ -191,6 +237,7 @@
             blocks = [amps[r * parts + s] for r in range(inner_size) if r or s]
             if s == 0:
                 *products, left_all = call(
+                    "products0",
                     functools.partial(first_products_kernel, inner_size, parts),
                     (kept, *blocks, *lefts),
                     [VMEM] * (inner_size + 3),
@@ -200,6 +247,7 @@
                 )
             else:
                 products = call(
+                    f"products{s}",
                     functools.partial(next_products_kernel, inner_size, parts),
                     (*blocks, left_all),
                     [VMEM] * (inner_size + 1),
@@ -212,21 +260,35 @@
             mine += [swap(products[2 * p], p, "inner", inner_size) for p in range(1, inner_size)]
             other = [swap(part, 1) for part in mine]
             crossed_other = [swap(part, 1) for part in crossed]
-            operands = (mask, *mine, *other, *crossed, *crossed_other)
+            operands = (weights, *mine, *other, *crossed, *crossed_other)
             made = call(
+                f"totals{s}",
                 functools.partial(totals_kernel, inner_size, right_tiles),
                 operands,
                 [VMEM] * len(operands),
-                [jax.ShapeDtypeStruct((right_tiles, 2, 2 * rows, depth), jnp.bfloat16)] * half,
+                [pltpu.VMEM((right_tiles, 2, 2 * rows, depth), jnp.bfloat16)] * half,
             )
             arrived += [made[0]] + [swap(made[m], 2 * m) for m in range(1, half)]
 
+        result_shape = (occupied_shift.shape[0], out_width)
+        inverse = call(
+            "inverse",
+            inverse_kernel,
+            (occupied_shift.reshape(1, -1), virtual_shift.reshape(1, -1)),
+            [VMEM] * 2,
+            pltpu.VMEM(result_shape, jnp.float32),
+        )
         return call(
+            "residual",
             functools.partial(residual_kernel, half, parts, z_half, rows),
-            (*arrived, right_factors, occupied_shift.reshape(-1, 1), virtual_shift.reshape(1, -1)),
-            [VMEM] * (len(arrived) + 3),
-            jax.ShapeDtypeStruct((occupied_shift.shape[0], out_width), jnp.float32),
-            (),
+            (*arrived, right_factors, inverse),
+            [VMEM] * (len(arrived) + 2),
+            jax.ShapeDtypeStruct(result_shape, jnp.float32),
+            [
+                pltpu.VMEM(result_shape, jnp.float32),
+                pltpu.VMEM((right_tiles, result_shape[0], right_factors.shape[0]), jnp.bfloat16),
+                pltpu.SemaphoreType.DMA((right_tiles,)),
+            ],
             2 * occupied_shift.shape[0] * out_width * right_factors.shape[0],
             4 << 20,
         )

time: 61.8 us -> 62.4 us (level)
  starting transfers between devices: 25.5 us -> 26.5 us
  Pallas kernels: 4.64 us -> 3.71 us
    pallas_call x6 -> x8, Pallas kernels: 4.64 us -> 3.71 us  [call(): pl.pallas_call(kernel, out_shape=out_shape, in_specs=in_specs, out_specs=...]
    ppermute x22, starting transfers between devices: 18.6 us -> 19.5 us  [swap(): return lax.ppermute(value, axis, [(t, t ^ q) for t in range(size)])]
  transfers between devices with their start and end apart: 26 -> 26, of which waited for: 12 -> 13; matrix products, arithmetic and copies ran while one was open for 0% -> 0% of each run, Pallas kernels for 4% -> 3%
where the time goes in v1:
time: 62.4 us; the launch traced here: 62.2 us
  waiting for transfers between devices  29.9 us (48%)
  starting transfers between devices  26.5 us (42%)
  Pallas kernels  3.71 us (6%)
  local copies, waits for them, and re-layouts  1.96 us (3%)
    ppermute x22, waiting for transfers between devices, swap(): return lax.ppermute(value, axis, [(t, t ^ q) for t in range(size)])  23.8 us
    ppermute x22, starting transfers between devices, swap(): return lax.ppermute(value, axis, [(t, t ^ q) for t in range(size)])  19.5 us
    ppermute x4, starting transfers between devices, cross(): return lax.ppermute(value, ('tile', 'inner'), pairs)  7.07 us
    ppermute x4, waiting for transfers between devices, cross(): return lax.ppermute(value, ('tile', 'inner'), pairs)  6.06 us
    pallas_call x8, Pallas kernels, call(): pl.pallas_call(kernel, out_shape=out_shape, in_specs=in_specs, out_specs=...  3.71 us
    unnamed x12, local copies, waits for them, and re-layouts  1.87 us
  transfers between devices with their start and end apart: 26, of which 13 were waited for; matrix products, arithmetic and copies ran while one was open for 0% of the time, Pallas kernels for 3%

profile of v1, /device:TPU:0, one launch (start us, length us, event | category | flops | bytes accessed | tf_op | source)
XLA Modules:
  0.0 62.2 jit_solution(12678196751857862058)
XLA Ops:
  0.0 3.0 %collective-permute-start.2 = (bf16[64,2048]{1,0:T(8,128)(2,1)}, bf16[64,2048]{1,0:T(8,128)(2,1)S(1)}, u32[]{:S(2)}, u32[]{:S(2)}) collective-permute-start(bf16[64,2048]{1,0:T(8,128)(2,1)} %left.1), channel_id=1, source_target_pairs={{0,4},{2,6},{4,0},{6,2},{8,12},{10,14},{12,8},{14,10},{16,20},{18,... | collective-permute-start | bytes 786440 | tf_op jit(solution)/shard_map/ppermute | solution.py:173
  3.0 0.0 collective-permute-start.1
  3.0 6.5 %collective-permute-done.2.refs_2_ = bf16[64,2048]{1,0:T(8,128)(2,1)S(1)} collective-permute-done((bf16[64,2048]{1,0:T(8,128)(2,1)}, bf16[64,2048]{1,0:T(8,128)(2,1)S(1)}, u32[]{:S(2)}, u32[]{:S(2)}) %collective-permute-start.2) | collective-permute-done | bytes 262176 | tf_op jit(solution)/shard_map/ppermute | solution.py:173
  9.5 0.0 collective-permute-start.3
  9.5 2.8 %collective-permute-start = (bf16[32,2048]{1,0:T(8,128)(2,1)}, bf16[32,2048]{1,0:T(8,128)(2,1)S(1)}, u32[]{:S(2)}, u32[]{:S(2)}) collective-permute-start(bf16[32,2048]{1,0:T(8,128)(2,1)} %amplitudes.1), channel_id=1, source_target_pairs={{0,16},{2,18},{4,20},{6,22},{8,24},{10,26},{12,28},{14,30},{16,0},... | collective-permute-start | bytes 393224 | tf_op jit(solution)/shard_map/ppermute | solution.py:173
  12.3 1.6 %collective-permute-start.14 = (bf16[32,2048]{1,0:T(8,128)(2,1)}, bf16[32,2048]{1,0:T(8,128)(2,1)S(1)}, u32[]{:S(2)}, u32[]{:S(2)}) collective-permute-start(bf16[32,2048]{1,0:T(8,128)(2,1)} %amplitudes.1), channel_id=1, source_target_pairs={{0,8},{2,10},{4,12},{6,14},{8,0},{10,2},{12,4},{14,6},{16,24},{18,... | collective-permute-start | bytes 393224 | tf_op jit(solution)/shard_map/ppermute | solution.py:173
  13.9 5.7 %collective-permute-done.refs_0_ = bf16[32,2048]{1,0:T(8,128)(2,1)S(1)} collective-permute-done((bf16[32,2048]{1,0:T(8,128)(2,1)}, bf16[32,2048]{1,0:T(8,128)(2,1)S(1)}, u32[]{:S(2)}, u32[]{:S(2)}) %collective-permute-start) | collective-permute-done | bytes 131104 | tf_op jit(solution)/shard_map/ppermute | solution.py:173
  19.6 0.7 %collective-permute-start.15 = (bf16[32,2048]{1,0:T(8,128)(2,1)S(1)}, bf16[32,2048]{1,0:T(8,128)(2,1)S(1)}, u32[]{:S(2)}, u32[]{:S(2)}) collective-permute-start(bf16[32,2048]{1,0:T(8,128)(2,1)S(1)} %collective-permute-done.refs_0_), channel_id=1, source_target_pairs={{0,8},{2,10},{4,12},{6,14},{8,0},{10,2},{12,4},{14,6},{16,24},{18,... | collective-permute-start | bytes 393224 | tf_op jit(solution)/shard_map/ppermute | solution.py:173
  20.3 0.9 %copy-done.1 = bf16[64,2048]{1,0:T(8,128)(2,1)S(1)} copy-done((bf16[64,2048]{1,0:T(8,128)(2,1)S(1)}, bf16[64,2048]{1,0:T(8,128)(2,1)}, u32[]{:S(2)}) %copy-start.1) | copy-done | bytes 262168
  21.3 0.9 %copy-done.2 = bf16[32,2048]{1,0:T(8,128)(2,1)S(1)} copy-done((bf16[32,2048]{1,0:T(8,128)(2,1)S(1)}, bf16[32,2048]{1,0:T(8,128)(2,1)}, u32[]{:S(2)}) %copy-start.2) | copy-done | bytes 131096
  22.2 0.0 collective-permute-done.1.refs_1_
  22.2 0.0 collective-permute-done.3.refs_3_
  22.2 0.6 shard_map.66
  22.8 0.0 copy-start.3
  22.8 0.0 copy-start.4
  22.8 0.0 collective-permute-done.14.refs_0_
  22.9 1.9 %collective-permute-done.15.refs_1_ = bf16[32,2048]{1,0:T(8,128)(2,1)S(1)} collective-permute-done((bf16[32,2048]{1,0:T(8,128)(2,1)S(1)}, bf16[32,2048]{1,0:T(8,128)(2,1)S(1)}, u32[]{:S(2)}, u32[]{:S(2)}) %collective-permute-start.15) | collective-permute-done | bytes 131104 | tf_op jit(solution)/shard_map/ppermute | solution.py:173
  24.7 0.5 shard_map.68
  25.2 2.7 %collective-permute-start.19 = (bf16[4,32,256]{2,1,0:T(8,128)(2,1)S(1)}, bf16[4,32,256]{2,1,0:T(8,128)(2,1)S(1)}, u32[]{:S(2)}, u32[]{:S(2)}) collective-permute-start(bf16[4,32,256]{2,1,0:T(8,128)(2,1)S(1)} %get-tuple-element.33), channel_id=1, source_target_pairs={{0,16},{1,17},{2,18},{3,19},{4,20},{5,21},{6,22},{7,23},{8,24},{9,... | collective-permute-start | bytes 196616 | tf_op jit(solution)/shard_map/ppermute | solution.py:181
  27.9 1.1 %collective-permute-start.20 = (bf16[4,32,256]{2,1,0:T(8,128)(2,1)S(1)}, bf16[4,32,256]{2,1,0:T(8,128)(2,1)S(1)}, u32[]{:S(2)}, u32[]{:S(2)}) collective-permute-start(bf16[4,32,256]{2,1,0:T(8,128)(2,1)S(1)} %get-tuple-element.34), channel_id=1, source_target_pairs={{0,17},{1,16},{2,19},{3,18},{4,21},{5,20},{6,23},{7,22},{8,25},{9,... | collective-permute-start | bytes 196616 | tf_op jit(solution)/shard_map/ppermute | solution.py:181
  29.0 0.6 %collective-permute-start.16 = (f32[4,32,256]{2,1,0:T(8,128)S(1)}, f32[4,32,256]{2,1,0:T(8,128)S(1)}, u32[]{:S(2)}, u32[]{:S(2)}) collective-permute-start(f32[4,32,256]{2,1,0:T(8,128)S(1)} %get-tuple-element.32), channel_id=1, source_target_pairs={{0,1},{1,0},{2,3},{3,2},{4,5},{5,4},{6,7},{7,6},{8,9},{9,8},{10,11... | collective-permute-start | bytes 393224 | tf_op jit(solution)/shard_map/ppermute | solution.py:173
  29.7 0.9 %collective-permute-done.19.refs_4_ = bf16[4,32,256]{2,1,0:T(8,128)(2,1)S(1)} collective-permute-done((bf16[4,32,256]{2,1,0:T(8,128)(2,1)S(1)}, bf16[4,32,256]{2,1,0:T(8,128)(2,1)S(1)}, u32[]{:S(2)}, u32[]{:S(2)}) %collective-permute-start.19) | collective-permute-done | bytes 65568 | tf_op jit(solution)/shard_map/ppermute | solution.py:181
  30.5 0.0 collective-permute-start.21
  30.5 3.9 %collective-permute-done.20.refs_5_ = bf16[4,32,256]{2,1,0:T(8,128)(2,1)S(1)} collective-permute-done((bf16[4,32,256]{2,1,0:T(8,128)(2,1)S(1)}, bf16[4,32,256]{2,1,0:T(8,128)(2,1)S(1)}, u32[]{:S(2)}, u32[]{:S(2)}) %collective-permute-start.20) | collective-permute-done | bytes 65568 | tf_op jit(solution)/shard_map/ppermute | solution.py:181
  34.4 0.0 collective-permute-start.22
  34.4 0.5 collective-permute-start.17
  34.9 1.1 %collective-permute-start.4 = (f32[4,32,256]{2,1,0:T(8,128)S(1)}, f32[4,32,256]{2,1,0:T(8,128)S(1)}, u32[]{:S(2)}, u32[]{:S(2)}) collective-permute-start(f32[4,32,256]{2,1,0:T(8,128)S(1)} %get-tuple-element.23), channel_id=1, source_target_pairs={{0,1},{1,0},{2,3},{3,2},{4,5},{5,4},{6,7},{7,6},{8,9},{9,8},{10,11... | collective-permute-start | bytes 393224 | tf_op jit(solution)/shard_map/ppermute | solution.py:173
  36.1 0.0 collective-permute-done.21.refs_6_
  36.1 0.7 %collective-permute-start.8 = (bf16[4,32,256]{2,1,0:T(8,128)(2,1)S(1)}, bf16[4,32,256]{2,1,0:T(8,128)(2,1)S(1)}, u32[]{:S(2)}, u32[]{:S(2)}) collective-permute-start(bf16[4,32,256]{2,1,0:T(8,128)(2,1)S(1)} %get-tuple-element.25), channel_id=1, source_target_pairs={{0,17},{1,16},{2,19},{3,18},{4,21},{5,20},{6,23},{7,22},{8,25},{9,... | collective-permute-start | bytes 196616 | tf_op jit(solution)/shard_map/ppermute | solution.py:181
  36.8 0.0 collective-permute-done.22.refs_7_
  36.8 2.5 %collective-permute-start.7 = (bf16[4,32,256]{2,1,0:T(8,128)(2,1)S(1)}, bf16[4,32,256]{2,1,0:T(8,128)(2,1)S(1)}, u32[]{:S(2)}, u32[]{:S(2)}) collective-permute-start(bf16[4,32,256]{2,1,0:T(8,128)(2,1)S(1)} %get-tuple-element.24), channel_id=1, source_target_pairs={{0,16},{1,17},{2,18},{3,19},{4,20},{5,21},{6,22},{7,23},{8,24},{9,... | collective-permute-start | bytes 196616 | tf_op jit(solution)/shard_map/ppermute | solution.py:181
  39.3 0.0 collective-permute-done.16.refs_1_
  39.3 0.0 collective-permute-start.18
  39.3 0.0 collective-permute-done.17.refs_2_
  39.3 0.6 collective-permute-start.5
  39.9 1.1 %collective-permute-done.4.refs_1_ = f32[4,32,256]{2,1,0:T(8,128)S(1)} collective-permute-done((f32[4,32,256]{2,1,0:T(8,128)S(1)}, f32[4,32,256]{2,1,0:T(8,128)S(1)}, u32[]{:S(2)}, u32[]{:S(2)}) %collective-permute-start.4) | collective-permute-done | bytes 131104 | tf_op jit(solution)/shard_map/ppermute | solution.py:173
  41.0 0.0 collective-permute-start.6
  41.0 0.1 broadcast_in_dim.2.mask
  41.1 0.1 shard_map.64.weights
  41.2 0.0 collective-permute-done.18.refs_3_
  41.2 0.4 shard_map.69
  41.6 1.6 %collective-permute-start.23 = (bf16[2,2,64,256]{3,2,1,0:T(8,128)(2,1)S(1)}, bf16[2,2,64,256]{3,2,1,0:T(8,128)(2,1)S(1)}, u32[]{:S(2)}, u32[]{:S(2)}) collective-permute-start(bf16[2,2,64,256]{3,2,1,0:T(8,128)(2,1)S(1)} %get-tuple-element.36), channel_id=1, source_target_pairs={{0,4},{2,6},{4,0},{6,2},{8,12},{10,14},{12,8},{14,10},{16,20},{18,... | collective-permute-start | bytes 393224 | tf_op jit(solution)/shard_map/ppermute | solution.py:173
  43.2 1.2 %collective-permute-done.8.refs_5_ = bf16[4,32,256]{2,1,0:T(8,128)(2,1)S(1)} collective-permute-done((bf16[4,32,256]{2,1,0:T(8,128)(2,1)S(1)}, bf16[4,32,256]{2,1,0:T(8,128)(2,1)S(1)}, u32[]{:S(2)}, u32[]{:S(2)}) %collective-permute-start.8) | collective-permute-done | bytes 65568 | tf_op jit(solution)/shard_map/ppermute | solution.py:181
  44.4 0.0 collective-permute-start.10
  44.4 0.1 collective-permute-done.7.refs_4_
  44.5 0.4 collective-permute-start.9
  44.9 0.7 %collective-permute-done.10.refs_7_ = bf16[4,32,256]{2,1,0:T(8,128)(2,1)S(1)} collective-permute-done((bf16[4,32,256]{2,1,0:T(8,128)(2,1)S(1)}, bf16[4,32,256]{2,1,0:T(8,128)(2,1)S(1)}, u32[]{:S(2)}, u32[]{:S(2)}) %collective-permute-start.10) | collective-permute-done | bytes 65568 | tf_op jit(solution)/shard_map/ppermute | solution.py:173
  45.6 0.5 collective-permute-start.24
  46.1 0.0 collective-permute-done.9.refs_6_
  46.1 2.5 %collective-permute-start.25 = (bf16[2,2,64,256]{3,2,1,0:T(8,128)(2,1)S(1)}, bf16[2,2,64,256]{3,2,1,0:T(8,128)(2,1)S(1)}, u32[]{:S(2)}, u32[]{:S(2)}) collective-permute-start(bf16[2,2,64,256]{3,2,1,0:T(8,128)(2,1)S(1)} %get-tuple-element.38), channel_id=1, source_target_pairs={{0,12},{2,14},{4,8},{6,10},{8,4},{10,6},{12,0},{14,2},{16,28},{18,... | collective-permute-start | bytes 393224 | tf_op jit(solution)/shard_map/ppermute | solution.py:173
  48.6 0.0 collective-permute-done.5.refs_2_
  48.6 0.0 collective-permute-done.6.refs_3_
  48.6 0.4 shard_map.67
  49.0 0.6 collective-permute-start.11
  49.6 0.5 collective-permute-start.12
  50.1 0.0 collective-permute-done.23.refs_5_
  50.1 2.5 %collective-permute-start.13 = (bf16[2,2,64,256]{3,2,1,0:T(8,128)(2,1)S(1)}, bf16[2,2,64,256]{3,2,1,0:T(8,128)(2,1)S(1)}, u32[]{:S(2)}, u32[]{:S(2)}) collective-permute-start(bf16[2,2,64,256]{3,2,1,0:T(8,128)(2,1)S(1)} %get-tuple-element.29), channel_id=1, source_target_pairs={{0,12},{2,14},{4,8},{6,10},{8,4},{10,6},{12,0},{14,2},{16,28},{18,... | collective-permute-start | bytes 393224 | tf_op jit(solution)/shard_map/ppermute | solution.py:173
  52.6 0.2 shard_map.70.refs_9_
  52.8 0.0 collective-permute-done.24.refs_6_
  52.8 3.0 %collective-permute-done.25.refs_7_ = bf16[2,2,64,256]{3,2,1,0:T(8,128)(2,1)S(1)} collective-permute-done((bf16[2,2,64,256]{3,2,1,0:T(8,128)(2,1)S(1)}, bf16[2,2,64,256]{3,2,1,0:T(8,128)(2,1)S(1)}, u32[]{:S(2)}, u32[]{:S(2)}) %collective-permute-start.25) | collective-permute-done | bytes 131104 | tf_op jit(solution)/shard_map/ppermute | solution.py:173
  55.8 1.1 %collective-permute-done.11.refs_1_ = bf16[2,2,64,256]{3,2,1,0:T(8,128)(2,1)S(1)} collective-permute-done((bf16[2,2,64,256]{3,2,1,0:T(8,128)(2,1)S(1)}, bf16[2,2,64,256]{3,2,1,0:T(8,128)(2,1)S(1)}, u32[]{:S(2)}, u32[]{:S(2)}) %collective-permute-start.11) | collective-permute-done | bytes 131104 | tf_op jit(solution)/shard_map/ppermute | solution.py:173
  56.9 0.8 %collective-permute-done.12.refs_2_ = bf16[2,2,64,256]{3,2,1,0:T(8,128)(2,1)S(1)} collective-permute-done((bf16[2,2,64,256]{3,2,1,0:T(8,128)(2,1)S(1)}, bf16[2,2,64,256]{3,2,1,0:T(8,128)(2,1)S(1)}, u32[]{:S(2)}, u32[]{:S(2)}) %collective-permute-start.12) | collective-permute-done | bytes 131104 | tf_op jit(solution)/shard_map/ppermute | solution.py:173
  57.7 3.0 %collective-permute-done.13.refs_3_ = bf16[2,2,64,256]{3,2,1,0:T(8,128)(2,1)S(1)} collective-permute-done((bf16[2,2,64,256]{3,2,1,0:T(8,128)(2,1)S(1)}, bf16[2,2,64,256]{3,2,1,0:T(8,128)(2,1)S(1)}, u32[]{:S(2)}, u32[]{:S(2)}) %collective-permute-start.13) | collective-permute-done | bytes 131104 | tf_op jit(solution)/shard_map/ppermute | solution.py:173
  60.6 1.6 %shard_map.71 = f32[256,1024]{1,0:T(8,128)} custom-call(bf16[2,2,64,256]{3,2,1,0:T(8,128)(2,1)S(1)} %get-tuple-element.26.refs_0_, bf16[2,2,64,256]{3,2,1,0:T(8,128)(2,1)S(1)} %collective-permute-done.11.refs_1_, bf16[2,2,64,256]{3,2,1,0:T(8,128)(2,1)S(1)} %collective-permute-done.12.refs_2_, bf16[2,2,64,256]{3,2,1,0:T(8,128)(2,1)S(1)} %collective-permute-done.13.refs_3_, ...), custom_call_target="tpu_custom_call" | custom-call | flops 536870912 | bytes 4194304 | tf_op jit(solution)/shard_map/pallas_call | solution.py:185
  (10 shorter events, 0.0 us)
Async XLA Ops:
  0.0 9.5 %collective-permute-start.2 = (bf16[64,2048]{1,0:T(8,128)(2,1)}, bf16[64,2048]{1,0:T(8,128)(2,1)S(1)}, u32[]{:S(2)}, u32[]{:S(2)}) collective-permute-start(bf16[64,2048]{1,0:T(8,128)(2,1)} %left.1), channel_id=1, source_target_pairs={{0,4},{2,6},{4,0},{6,2},{8,12},{10,14},{12,8},{14,10},{16,20},{18,... | collective-permute-start | bytes 786440 | tf_op jit(solution)/shard_map/ppermute | solution.py:173
  3.0 19.2 %collective-permute-start.1 = (bf16[64,2048]{1,0:T(8,128)(2,1)}, bf16[64,2048]{1,0:T(8,128)(2,1)S(1)}, u32[]{:S(2)}, u32[]{:S(2)}) collective-permute-start(bf16[64,2048]{1,0:T(8,128)(2,1)} %left.1), channel_id=1, source_target_pairs={{0,2},{2,0},{4,6},{6,4},{8,10},{10,8},{12,14},{14,12},{16,18},{18,... | collective-permute-start | bytes 786440 | tf_op jit(solution)/shard_map/ppermute | solution.py:173
  9.5 12.7 %collective-permute-start.3 = (bf16[64,2048]{1,0:T(8,128)(2,1)S(1)}, bf16[64,2048]{1,0:T(8,128)(2,1)S(1)}, u32[]{:S(2)}, u32[]{:S(2)}) collective-permute-start(bf16[64,2048]{1,0:T(8,128)(2,1)S(1)} %collective-permute-done.2.refs_2_), channel_id=1, source_target_pairs={{0,2},{2,0},{4,6},{6,4},{8,10},{10,8},{12,14},{14,12},{16,18},{18,... | collective-permute-start | bytes 786440 | tf_op jit(solution)/shard_map/ppermute | solution.py:173
  9.5 10.1 %collective-permute-start = (bf16[32,2048]{1,0:T(8,128)(2,1)}, bf16[32,2048]{1,0:T(8,128)(2,1)S(1)}, u32[]{:S(2)}, u32[]{:S(2)}) collective-permute-start(bf16[32,2048]{1,0:T(8,128)(2,1)} %amplitudes.1), channel_id=1, source_target_pairs={{0,16},{2,18},{4,20},{6,22},{8,24},{10,26},{12,28},{14,30},{16,0},... | collective-permute-start | bytes 393224 | tf_op jit(solution)/shard_map/ppermute | solution.py:173
  12.3 10.5 %collective-permute-start.14 = (bf16[32,2048]{1,0:T(8,128)(2,1)}, bf16[32,2048]{1,0:T(8,128)(2,1)S(1)}, u32[]{:S(2)}, u32[]{:S(2)}) collective-permute-start(bf16[32,2048]{1,0:T(8,128)(2,1)} %amplitudes.1), channel_id=1, source_target_pairs={{0,8},{2,10},{4,12},{6,14},{8,0},{10,2},{12,4},{14,6},{16,24},{18,... | collective-permute-start | bytes 393224 | tf_op jit(solution)/shard_map/ppermute | solution.py:173
  19.6 5.1 %collective-permute-start.15 = (bf16[32,2048]{1,0:T(8,128)(2,1)S(1)}, bf16[32,2048]{1,0:T(8,128)(2,1)S(1)}, u32[]{:S(2)}, u32[]{:S(2)}) collective-permute-start(bf16[32,2048]{1,0:T(8,128)(2,1)S(1)} %collective-permute-done.refs_0_), channel_id=1, source_target_pairs={{0,8},{2,10},{4,12},{6,14},{8,0},{10,2},{12,4},{14,6},{16,24},{18,... | collective-permute-start | bytes 393224 | tf_op jit(solution)/shard_map/ppermute | solution.py:173
  20.3 0.9 %copy-start.1 = (bf16[64,2048]{1,0:T(8,128)(2,1)S(1)}, bf16[64,2048]{1,0:T(8,128)(2,1)}, u32[]{:S(2)}) copy-start(bf16[64,2048]{1,0:T(8,128)(2,1)} %left.1) | copy-start | bytes 786436
  21.3 0.9 %copy-start.2 = (bf16[32,2048]{1,0:T(8,128)(2,1)S(1)}, bf16[32,2048]{1,0:T(8,128)(2,1)}, u32[]{:S(2)}) copy-start(bf16[32,2048]{1,0:T(8,128)(2,1)} %amplitudes.1) | copy-start | bytes 393220
  22.2 17.1 %copy-start.5 = (s32[8,32]{1,0:T(8,128)S(1)}, s32[8,32]{1,0:T(8,128)}, u32[]{:S(2)}) copy-start(s32[8,32]{1,0:T(8,128)} %param.9) | copy-start | bytes 3076
  22.8 29.8 %copy-start.3 = (f32[1024]{0:T(1024)S(1)}, f32[1024]{0:T(1024)}, u32[]{:S(2)}) copy-start(f32[1024]{0:T(1024)} %param.11) | copy-start | bytes 12292
  22.8 29.8 %copy-start.4 = (f32[256]{0:T(256)S(1)}, f32[256]{0:T(256)}, u32[]{:S(2)}) copy-start(f32[256]{0:T(256)} %param.10) | copy-start | bytes 3076
  24.7 35.9 %copy-start = (bf16[1024,1024]{1,0:T(8,128)(2,1)S(1)}, bf16[1024,1024]{1,0:T(8,128)(2,1)}, u32[]{:S(2)}) copy-start(bf16[1024,1024]{1,0:T(8,128)(2,1)} %refs_8_.1) | copy-start | bytes 6291460
  25.2 5.3 %collective-permute-start.19 = (bf16[4,32,256]{2,1,0:T(8,128)(2,1)S(1)}, bf16[4,32,256]{2,1,0:T(8,128)(2,1)S(1)}, u32[]{:S(2)}, u32[]{:S(2)}) collective-permute-start(bf16[4,32,256]{2,1,0:T(8,128)(2,1)S(1)} %get-tuple-element.33), channel_id=1, source_target_pairs={{0,16},{1,17},{2,18},{3,19},{4,20},{5,21},{6,22},{7,23},{8,24},{9,... | collective-permute-start | bytes 196616 | tf_op jit(solution)/shard_map/ppermute | solution.py:181
  27.9 6.5 %collective-permute-start.20 = (bf16[4,32,256]{2,1,0:T(8,128)(2,1)S(1)}, bf16[4,32,256]{2,1,0:T(8,128)(2,1)S(1)}, u32[]{:S(2)}, u32[]{:S(2)}) collective-permute-start(bf16[4,32,256]{2,1,0:T(8,128)(2,1)S(1)} %get-tuple-element.34), channel_id=1, source_target_pairs={{0,17},{1,16},{2,19},{3,18},{4,21},{5,20},{6,23},{7,22},{8,25},{9,... | collective-permute-start | bytes 196616 | tf_op jit(solution)/shard_map/ppermute | solution.py:181
  29.0 10.3 %collective-permute-start.16 = (f32[4,32,256]{2,1,0:T(8,128)S(1)}, f32[4,32,256]{2,1,0:T(8,128)S(1)}, u32[]{:S(2)}, u32[]{:S(2)}) collective-permute-start(f32[4,32,256]{2,1,0:T(8,128)S(1)} %get-tuple-element.32), channel_id=1, source_target_pairs={{0,1},{1,0},{2,3},{3,2},{4,5},{5,4},{6,7},{7,6},{8,9},{9,8},{10,11... | collective-permute-start | bytes 393224 | tf_op jit(solution)/shard_map/ppermute | solution.py:173
  30.5 5.5 %collective-permute-start.21 = (bf16[4,32,256]{2,1,0:T(8,128)(2,1)S(1)}, bf16[4,32,256]{2,1,0:T(8,128)(2,1)S(1)}, u32[]{:S(2)}, u32[]{:S(2)}) collective-permute-start(bf16[4,32,256]{2,1,0:T(8,128)(2,1)S(1)} %collective-permute-done.19.refs_4_), channel_id=1, source_target_pairs={{0,2},{2,0},{4,6},{6,4},{8,10},{10,8},{12,14},{14,12},{16,18},{18,... | collective-permute-start | bytes 196616 | tf_op jit(solution)/shard_map/ppermute | solution.py:173
  34.4 2.4 %collective-permute-start.22 = (bf16[4,32,256]{2,1,0:T(8,128)(2,1)S(1)}, bf16[4,32,256]{2,1,0:T(8,128)(2,1)S(1)}, u32[]{:S(2)}, u32[]{:S(2)}) collective-permute-start(bf16[4,32,256]{2,1,0:T(8,128)(2,1)S(1)} %collective-permute-done.20.refs_5_), channel_id=1, source_target_pairs={{0,2},{2,0},{4,6},{6,4},{8,10},{10,8},{12,14},{14,12},{16,18},{18,... | collective-permute-start | bytes 196616 | tf_op jit(solution)/shard_map/ppermute | solution.py:173
  34.4 4.9 %collective-permute-start.17 = (f32[4,32,256]{2,1,0:T(8,128)S(1)}, f32[4,32,256]{2,1,0:T(8,128)S(1)}, u32[]{:S(2)}, u32[]{:S(2)}) collective-permute-start(f32[4,32,256]{2,1,0:T(8,128)S(1)} %get-tuple-element.31.refs_0_), channel_id=1, source_target_pairs={{0,2},{2,0},{4,6},{6,4},{8,10},{10,8},{12,14},{14,12},{16,18},{18,... | collective-permute-start | bytes 393224 | tf_op jit(solution)/shard_map/ppermute | solution.py:173
  34.9 6.1 %collective-permute-start.4 = (f32[4,32,256]{2,1,0:T(8,128)S(1)}, f32[4,32,256]{2,1,0:T(8,128)S(1)}, u32[]{:S(2)}, u32[]{:S(2)}) collective-permute-start(f32[4,32,256]{2,1,0:T(8,128)S(1)} %get-tuple-element.23), channel_id=1, source_target_pairs={{0,1},{1,0},{2,3},{3,2},{4,5},{5,4},{6,7},{7,6},{8,9},{9,8},{10,11... | collective-permute-start | bytes 393224 | tf_op jit(solution)/shard_map/ppermute | solution.py:173
  36.1 8.3 %collective-permute-start.8 = (bf16[4,32,256]{2,1,0:T(8,128)(2,1)S(1)}, bf16[4,32,256]{2,1,0:T(8,128)(2,1)S(1)}, u32[]{:S(2)}, u32[]{:S(2)}) collective-permute-start(bf16[4,32,256]{2,1,0:T(8,128)(2,1)S(1)} %get-tuple-element.25), channel_id=1, source_target_pairs={{0,17},{1,16},{2,19},{3,18},{4,21},{5,20},{6,23},{7,22},{8,25},{9,... | collective-permute-start | bytes 196616 | tf_op jit(solution)/shard_map/ppermute | solution.py:181
  36.8 7.7 %collective-permute-start.7 = (bf16[4,32,256]{2,1,0:T(8,128)(2,1)S(1)}, bf16[4,32,256]{2,1,0:T(8,128)(2,1)S(1)}, u32[]{:S(2)}, u32[]{:S(2)}) collective-permute-start(bf16[4,32,256]{2,1,0:T(8,128)(2,1)S(1)} %get-tuple-element.24), channel_id=1, source_target_pairs={{0,16},{1,17},{2,18},{3,19},{4,20},{5,21},{6,22},{7,23},{8,24},{9,... | collective-permute-start | bytes 196616 | tf_op jit(solution)/shard_map/ppermute | solution.py:181
  39.3 1.9 %collective-permute-start.18 = (f32[4,32,256]{2,1,0:T(8,128)S(1)}, f32[4,32,256]{2,1,0:T(8,128)S(1)}, u32[]{:S(2)}, u32[]{:S(2)}) collective-permute-start(f32[4,32,256]{2,1,0:T(8,128)S(1)} %collective-permute-done.16.refs_1_), channel_id=1, source_target_pairs={{0,2},{2,0},{4,6},{6,4},{8,10},{10,8},{12,14},{14,12},{16,18},{18,... | collective-permute-start | bytes 393224 | tf_op jit(solution)/shard_map/ppermute | solution.py:173
  39.3 9.3 %collective-permute-start.5 = (f32[4,32,256]{2,1,0:T(8,128)S(1)}, f32[4,32,256]{2,1,0:T(8,128)S(1)}, u32[]{:S(2)}, u32[]{:S(2)}) collective-permute-start(f32[4,32,256]{2,1,0:T(8,128)S(1)} %get-tuple-element.22.refs_0_), channel_id=1, source_target_pairs={{0,2},{2,0},{4,6},{6,4},{8,10},{10,8},{12,14},{14,12},{16,18},{18,... | collective-permute-start | bytes 393224 | tf_op jit(solution)/shard_map/ppermute | solution.py:173
  41.0 7.6 %collective-permute-start.6 = (f32[4,32,256]{2,1,0:T(8,128)S(1)}, f32[4,32,256]{2,1,0:T(8,128)S(1)}, u32[]{:S(2)}, u32[]{:S(2)}) collective-permute-start(f32[4,32,256]{2,1,0:T(8,128)S(1)} %collective-permute-done.4.refs_1_), channel_id=1, source_target_pairs={{0,2},{2,0},{4,6},{6,4},{8,10},{10,8},{12,14},{14,12},{16,18},{18,... | collective-permute-start | bytes 393224 | tf_op jit(solution)/shard_map/ppermute | solution.py:173
  41.6 8.5 %collective-permute-start.23 = (bf16[2,2,64,256]{3,2,1,0:T(8,128)(2,1)S(1)}, bf16[2,2,64,256]{3,2,1,0:T(8,128)(2,1)S(1)}, u32[]{:S(2)}, u32[]{:S(2)}) collective-permute-start(bf16[2,2,64,256]{3,2,1,0:T(8,128)(2,1)S(1)} %get-tuple-element.36), channel_id=1, source_target_pairs={{0,4},{2,6},{4,0},{6,2},{8,12},{10,14},{12,8},{14,10},{16,20},{18,... | collective-permute-start | bytes 393224 | tf_op jit(solution)/shard_map/ppermute | solution.py:173
  44.4 1.3 %collective-permute-start.10 = (bf16[4,32,256]{2,1,0:T(8,128)(2,1)S(1)}, bf16[4,32,256]{2,1,0:T(8,128)(2,1)S(1)}, u32[]{:S(2)}, u32[]{:S(2)}) collective-permute-start(bf16[4,32,256]{2,1,0:T(8,128)(2,1)S(1)} %collective-permute-done.8.refs_5_), channel_id=1, source_target_pairs={{0,2},{2,0},{4,6},{6,4},{8,10},{10,8},{12,14},{14,12},{16,18},{18,... | collective-permute-start | bytes 196616 | tf_op jit(solution)/shard_map/ppermute | solution.py:173
  44.5 1.6 %collective-permute-start.9 = (bf16[4,32,256]{2,1,0:T(8,128)(2,1)S(1)}, bf16[4,32,256]{2,1,0:T(8,128)(2,1)S(1)}, u32[]{:S(2)}, u32[]{:S(2)}) collective-permute-start(bf16[4,32,256]{2,1,0:T(8,128)(2,1)S(1)} %collective-permute-done.7.refs_4_), channel_id=1, source_target_pairs={{0,2},{2,0},{4,6},{6,4},{8,10},{10,8},{12,14},{14,12},{16,18},{18,... | collective-permute-start | bytes 196616 | tf_op jit(solution)/shard_map/ppermute | solution.py:173
  45.6 7.2 %collective-permute-start.24 = (bf16[2,2,64,256]{3,2,1,0:T(8,128)(2,1)S(1)}, bf16[2,2,64,256]{3,2,1,0:T(8,128)(2,1)S(1)}, u32[]{:S(2)}, u32[]{:S(2)}) collective-permute-start(bf16[2,2,64,256]{3,2,1,0:T(8,128)(2,1)S(1)} %get-tuple-element.37), channel_id=1, source_target_pairs={{0,8},{2,10},{4,12},{6,14},{8,0},{10,2},{12,4},{14,6},{16,24},{18,... | collective-permute-start | bytes 393224 | tf_op jit(solution)/shard_map/ppermute | solution.py:173
  46.1 9.7 %collective-permute-start.25 = (bf16[2,2,64,256]{3,2,1,0:T(8,128)(2,1)S(1)}, bf16[2,2,64,256]{3,2,1,0:T(8,128)(2,1)S(1)}, u32[]{:S(2)}, u32[]{:S(2)}) collective-permute-start(bf16[2,2,64,256]{3,2,1,0:T(8,128)(2,1)S(1)} %get-tuple-element.38), channel_id=1, source_target_pairs={{0,12},{2,14},{4,8},{6,10},{8,4},{10,6},{12,0},{14,2},{16,28},{18,... | collective-permute-start | bytes 393224 | tf_op jit(solution)/shard_map/ppermute | solution.py:173
  49.0 7.9 %collective-permute-start.11 = (bf16[2,2,64,256]{3,2,1,0:T(8,128)(2,1)S(1)}, bf16[2,2,64,256]{3,2,1,0:T(8,128)(2,1)S(1)}, u32[]{:S(2)}, u32[]{:S(2)}) collective-permute-start(bf16[2,2,64,256]{3,2,1,0:T(8,128)(2,1)S(1)} %get-tuple-element.27), channel_id=1, source_target_pairs={{0,4},{2,6},{4,0},{6,2},{8,12},{10,14},{12,8},{14,10},{16,20},{18,... | collective-permute-start | bytes 393224 | tf_op jit(solution)/shard_map/ppermute | solution.py:173
  49.6 8.1 %collective-permute-start.12 = (bf16[2,2,64,256]{3,2,1,0:T(8,128)(2,1)S(1)}, bf16[2,2,64,256]{3,2,1,0:T(8,128)(2,1)S(1)}, u32[]{:S(2)}, u32[]{:S(2)}) collective-permute-start(bf16[2,2,64,256]{3,2,1,0:T(8,128)(2,1)S(1)} %get-tuple-element.28), channel_id=1, source_target_pairs={{0,8},{2,10},{4,12},{6,14},{8,0},{10,2},{12,4},{14,6},{16,24},{18,... | collective-permute-start | bytes 393224 | tf_op jit(solution)/shard_map/ppermute | solution.py:173
  50.1 10.5 %collective-permute-start.13 = (bf16[2,2,64,256]{3,2,1,0:T(8,128)(2,1)S(1)}, bf16[2,2,64,256]{3,2,1,0:T(8,128)(2,1)S(1)}, u32[]{:S(2)}, u32[]{:S(2)}) collective-permute-start(bf16[2,2,64,256]{3,2,1,0:T(8,128)(2,1)S(1)} %get-tuple-element.29), channel_id=1, source_target_pairs={{0,12},{2,14},{4,8},{6,10},{8,4},{10,6},{12,0},{14,2},{16,28},{18,... | collective-permute-start | bytes 393224 | tf_op jit(solution)/shard_map/ppermute | solution.py:173
